TPU v7x, 32 devices: a whole 2x2x4 slice. The times are simulated.
32 devices in a mesh: dp: 8 (over y, x, core), mp: 4 (over z).
Axes of the slice: x: 2, y: 2, z: 4, core: 2. Of those that a mesh axis runs over, the one named last changes fastest.
Arguments:
- inputs: bfloat16 [16, 512, 1024], P('dp'), may hold values from -6 to 6
- memory: bfloat16 [16, 512, 1024], P('dp'), may hold values from -6 to 6
- compressed_memory: bfloat16 [16, 512, 1024], P('dp'), may hold values from -6 to 6
- memory_fill: int32 [16], P('dp'), may hold values from 0 to 512, as said below
- compressed_fill: int32 [16], P('dp'), may hold values from 0 to 512, as said below
- first_gain: float32 [1024], replicated, may hold values from 0.5 to 1.5
- query_weight: bfloat16 [1024, 1024], P(None, 'mp'), may hold values from -0.1875 to 0.1875
- key_weight: bfloat16 [1024, 1024], P(None, 'mp'), may hold values from -0.1875 to 0.1875
- value_weight: bfloat16 [1024, 1024], P(None, 'mp'), may hold values from -0.1875 to 0.1875
- relative_bias: float32 [8, 22], P('mp'), may hold values from -1.5 to 1.5
- output_weight: bfloat16 [1024, 1024], P('mp'), may hold values from -1.5 to 1.5
- second_gain: float32 [1024], replicated, may hold values from 0.5 to 1.5
- up_weight: bfloat16 [1024, 4096], P(None, 'mp'), may hold values from -0.1875 to 0.1875
- down_weight: bfloat16 [4096, 1024], P('mp'), may hold values from -0.09375 to 0.09375
- compress_weight: bfloat16 [2048, 1024], P(None, 'mp'), may hold values from -0.125 to 0.125
- grad_output: bfloat16 [16, 512, 1024], P('dp'), may hold values from -6 to 6
- grad_compressed: bfloat16 [16, 256, 1024], P('dp', None, 'mp'), may hold values from -6 to 6
Outputs:
- outputs: bfloat16 [16, 512, 1024], P('dp')
- compressed: bfloat16 [16, 256, 1024], P('dp', None, 'mp')
- grad_inputs: bfloat16 [16, 512, 1024], P('dp')
- grad_first_gain: float32 [1024], replicated
- grad_query: float32 [1024, 1024], P(None, 'mp')
- grad_key: float32 [1024, 1024], P(None, 'mp')
- grad_value: float32 [1024, 1024], P(None, 'mp')
- grad_relative: float32 [8, 22], P('mp')
- grad_output_weight: float32 [1024, 1024], P('mp')
- grad_second_gain: float32 [1024], replicated
- grad_up: float32 [1024, 4096], P(None, 'mp')
- grad_down: float32 [4096, 1024], P('mp')
- grad_compress: float32 [2048, 1024], P(None, 'mp')
Inputs may be any that keep to these rules, and one draw needn't show every extreme that they name: `memory_fill`: some stream has a full memory and some stream an empty one. `compressed_fill`: some stream has a full compressed memory and some stream an empty one.
All inputs are finite; a program needn't handle non-finite values.
Results may differ from a plain program's by a relative error of at most 0.023.
Values sent between devices are 32-bit elements; how exact they have to be, the bound alone decides.
A program may use at most 320 MiB of HBM per device.

v0:
```python
import math
import jax
import jax.numpy as jnp
from jax import lax
from jax.sharding import PartitionSpec as P

reach_marks = (
    1,
    2,
    3,
    4,
    5,
    6,
    7,
    8,
    12,
    16,
    24,
    32,
    48,
    64,
    96,
    128,
    192,
    256,
    384,
    512,
    768,
    1024,
)
epsilon = 1e-06


def rms_scale(source, gain):
    return source * lax.rsqrt(jnp.mean(source * source, axis=-1, keepdims=True) + epsilon) * gain


def low_product(left, right):
    return jnp.dot(left, right, preferred_element_type=jnp.float32)


def weight_grad(left, right):
    return lax.dot_general(
        left, right, (((0,), (0,)), ((), ())), preferred_element_type=jnp.float32
    )


def back_product(left, right):
    return lax.dot_general(
        left, right, (((1,), (1,)), ((), ())), preferred_element_type=jnp.float32
    )


def gelu_tanh(source):
    return jax.nn.gelu(source, approximate=True)


def body(
    inputs,
    memory,
    compressed_memory,
    memory_fill,
    compressed_fill,
    first_gain,
    query_weight,
    key_weight,
    value_weight,
    relative_bias,
    output_weight,
    second_gain,
    up_weight,
    down_weight,
    compress_weight,
    grad_output,
    grad_compressed,
):
    seg_len = inputs.shape[1]
    mem_len = memory.shape[1]
    packed_len = compressed_memory.shape[1]
    model_width = inputs.shape[2]
    kept_count = packed_len + mem_len
    key_count = kept_count + seg_len
    heads_here = relative_bias.shape[0]
    head_dim = query_weight.shape[1] // heads_here
    compress_count = grad_compressed.shape[1]
    score_scale = 1.0 / math.sqrt(head_dim)
    distance = (
        jnp.arange(seg_len, dtype=jnp.int32)[:, None]
        + kept_count
        - jnp.arange(key_count, dtype=jnp.int32)[None, :]
    )
    causal = distance >= 0
    bias_table = jnp.zeros((heads_here, seg_len, key_count), jnp.float32)
    for position, mark_value in enumerate(reach_marks):
        bias_table = (
            bias_table
            + relative_bias[:, position][:, None, None]
            * (distance >= mark_value).astype(jnp.float32)[None]
        )

    def split_heads(source):
        return source.reshape(source.shape[0], heads_here, head_dim)

    def score_grid(queries, key_rows, allowed):
        raw_scores = (
            jnp.einsum(
                "shd,khd->hsk",
                split_heads(queries),
                split_heads(key_rows),
                preferred_element_type=jnp.float32,
            )
            * score_scale
            + bias_table
        )
        return jnp.where(allowed[None], raw_scores, -1e30)

    def attend(seg_rows, memory_rows, packed_rows, memory_count, packed_count):
        stacked = jnp.concatenate([packed_rows, memory_rows, seg_rows], axis=0).astype(jnp.float32)
        unit_rows = rms_scale(stacked, first_gain).astype(jnp.bfloat16)
        queries = low_product(unit_rows[kept_count:], query_weight).astype(jnp.bfloat16)
        key_rows = low_product(unit_rows, key_weight).astype(jnp.bfloat16)
        value_rows = low_product(unit_rows, value_weight).astype(jnp.bfloat16)
        valid_keys = jnp.concatenate(
            [
                jnp.arange(packed_len, dtype=jnp.int32) >= packed_len - packed_count,
                jnp.arange(mem_len, dtype=jnp.int32) >= mem_len - memory_count,
                jnp.ones((seg_len,), jnp.bool_),
            ]
        )
        allowed = causal & valid_keys[None, :]
        masked = score_grid(queries, key_rows, allowed)
        top_score = jnp.max(masked, axis=-1, keepdims=True)
        log_total = top_score + jnp.log(
            jnp.sum(jnp.exp(masked - top_score), axis=-1, keepdims=True)
        )
        prob_low = jnp.exp(masked - log_total).astype(jnp.bfloat16)
        mixed_heads = jnp.einsum(
            "hsk,khd->shd", prob_low, split_heads(value_rows), preferred_element_type=jnp.float32
        )
        mixed_heads = mixed_heads.reshape(seg_len, heads_here * head_dim).astype(jnp.bfloat16)
        attended = lax.psum(low_product(mixed_heads, output_weight), "mp")
        residual = seg_rows.astype(jnp.float32) + attended
        return (
            stacked,
            unit_rows,
            queries,
            key_rows,
            value_rows,
            allowed,
            log_total,
            mixed_heads,
            residual,
        )

    def feed(residual):
        ffn_input = rms_scale(residual, second_gain).astype(jnp.bfloat16)
        pre_act = low_product(ffn_input, up_weight)
        activated = gelu_tanh(pre_act).astype(jnp.bfloat16)
        return (ffn_input, pre_act, activated)

    def stream_step(totals, stream_item):
        seg_rows, memory_rows, packed_rows, memory_count, packed_count, grad_rows, grad_packed = (
            stream_item
        )
        saved = attend(seg_rows, memory_rows, packed_rows, memory_count, packed_count)
        ffn_input, pre_act, activated = feed(saved[8])
        branch_out = lax.psum(low_product(activated, down_weight), "mp")
        result = (saved[8] + branch_out).astype(jnp.bfloat16)
        again = lax.optimization_barrier((seg_rows, memory_rows, packed_rows, result))
        saved = attend(again[0], again[1], again[2], memory_count, packed_count)
        ffn_input, pre_act, activated = feed(saved[8])
        (
            stacked,
            unit_rows,
            queries,
            key_rows,
            value_rows,
            allowed,
            log_total,
            mixed_heads,
            residual,
        ) = saved
        slot_index = jnp.arange(mem_len, dtype=jnp.int32)
        live_rows = jnp.where(
            (slot_index >= mem_len - memory_count)[:, None],
            memory_rows,
            jnp.zeros_like(memory_rows),
        )
        evicted = live_rows.reshape(compress_count, 2 * model_width)
        packed_new = low_product(evicted, compress_weight).astype(jnp.bfloat16)
        grad_down = weight_grad(activated, grad_rows)
        _, gelu_back = jax.vjp(gelu_tanh, pre_act)
        grad_pre = gelu_back(back_product(grad_rows, down_weight))[0].astype(jnp.bfloat16)
        grad_up = weight_grad(ffn_input, grad_pre)
        grad_ffn_input = lax.psum(back_product(grad_pre, up_weight), "mp")
        _, second_back = jax.vjp(rms_scale, residual, second_gain)
        grad_res_norm, grad_second = second_back(grad_ffn_input)
        grad_residual = grad_rows.astype(jnp.float32) + grad_res_norm
        grad_attended = grad_residual.astype(jnp.bfloat16)
        grad_out_weight = weight_grad(mixed_heads, grad_attended)
        grad_mixed = back_product(grad_attended, output_weight).astype(jnp.bfloat16)
        masked = score_grid(queries, key_rows, allowed)
        attend_prob = jnp.exp(masked - log_total)
        grad_prob = jnp.einsum(
            "shd,khd->hsk",
            split_heads(grad_mixed),
            split_heads(value_rows),
            preferred_element_type=jnp.float32,
        )
        grad_score = (
            attend_prob * (grad_prob - jnp.sum(grad_prob * attend_prob, axis=-1, keepdims=True))
        ).astype(jnp.bfloat16)
        score_wide = grad_score.astype(jnp.float32)
        grad_relative = jnp.stack(
            [
                jnp.sum(jnp.where((distance >= mark_value)[None], score_wide, 0.0), axis=(1, 2))
                for mark_value in reach_marks
            ],
            axis=1,
        )
        grad_queries = (
            (
                jnp.einsum(
                    "hsk,khd->shd",
                    grad_score,
                    split_heads(key_rows),
                    preferred_element_type=jnp.float32,
                )
                * score_scale
            )
            .reshape(seg_len, heads_here * head_dim)
            .astype(jnp.bfloat16)
        )
        grad_keys = (
            (
                jnp.einsum(
                    "hsk,shd->khd",
                    grad_score,
                    split_heads(queries),
                    preferred_element_type=jnp.float32,
                )
                * score_scale
            )
            .reshape(key_count, heads_here * head_dim)
            .astype(jnp.bfloat16)
        )
        grad_values = (
            jnp.einsum(
                "hsk,shd->khd",
                attend_prob.astype(jnp.bfloat16),
                split_heads(grad_mixed),
                preferred_element_type=jnp.float32,
            )
            .reshape(key_count, heads_here * head_dim)
            .astype(jnp.bfloat16)
        )
        grad_query_w = weight_grad(unit_rows[kept_count:], grad_queries)
        grad_key_w = weight_grad(unit_rows, grad_keys)
        grad_value_w = weight_grad(unit_rows, grad_values)
        grad_unit = back_product(grad_keys, key_weight) + back_product(grad_values, value_weight)
        grad_unit_seg = grad_unit[kept_count:] + back_product(grad_queries, query_weight)
        _, kept_back = jax.vjp(rms_scale, stacked[:kept_count], first_gain)
        grad_first_kept = kept_back(grad_unit[:kept_count])[1]
        grad_unit_seg, grad_first_kept = lax.psum((grad_unit_seg, grad_first_kept), "mp")
        _, seg_back = jax.vjp(rms_scale, stacked[kept_count:], first_gain)
        grad_seg_norm, grad_first_seg = seg_back(grad_unit_seg)
        grad_seg = (grad_residual + grad_seg_norm).astype(jnp.bfloat16)
        grad_compress_w = weight_grad(evicted, grad_packed)
        gradients = (
            grad_first_kept + grad_first_seg,
            grad_query_w,
            grad_key_w,
            grad_value_w,
            grad_relative,
            grad_out_weight,
            grad_second,
            grad_up,
            grad_down,
            grad_compress_w,
        )
        totals = tuple((total + grad_item for total, grad_item in zip(totals, gradients)))
        return (totals, (result, packed_new, grad_seg))

    initial = tuple(
        (
            jnp.zeros(item.shape, jnp.float32)
            for item in (
                first_gain,
                query_weight,
                key_weight,
                value_weight,
                relative_bias,
                output_weight,
                second_gain,
                up_weight,
                down_weight,
                compress_weight,
            )
        )
    )
    stream_items = (
        inputs,
        memory,
        compressed_memory,
        memory_fill,
        compressed_fill,
        grad_output,
        grad_compressed,
    )
    totals, (results, packed_all, grad_all) = lax.scan(stream_step, initial, stream_items)
    totals = lax.psum(totals, "dp")
    return (results, packed_all, grad_all) + tuple(totals)


def solution(mesh):
    in_specs = (
        P("dp", None, None),
        P("dp", None, None),
        P("dp", None, None),
        P("dp"),
        P("dp"),
        P(),
        P(None, "mp"),
        P(None, "mp"),
        P(None, "mp"),
        P("mp", None),
        P("mp", None),
        P(),
        P(None, "mp"),
        P("mp", None),
        P(None, "mp"),
        P("dp", None, None),
        P("dp", None, "mp"),
    )
    out_specs = (
        P("dp", None, None),
        P("dp", None, "mp"),
        P("dp", None, None),
        P(),
        P(None, "mp"),
        P(None, "mp"),
        P(None, "mp"),
        P("mp", None),
        P("mp", None),
        P(),
        P(None, "mp"),
        P("mp", None),
        P(None, "mp"),
    )
    return jax.shard_map(body, mesh=mesh, in_specs=in_specs, out_specs=out_specs, check_vma=False)
```

profile of v0, /device:TPU:0, one launch (start us, length us, event | category | flops | bytes accessed | tf_op | source)
XLA Modules:
  0.0 1445.7 jit_solution(14084164727525014909)
XLA Ops:
  11.6 22.1 %fusion.144 = (f32[512,1536]{1,0:T(8,128)}, f32[512,1536]{1,0:T(8,128)}, f32[512,1536]{1,0:T(8,128)}, f32[512,1536]{1,0:T(8,128)}, f32[512,1536]{1,0:T(8,128)}, ...) fusion(s32[512]{0:T(512)S(1)} %iota_add_fusion), kind=kLoop, calls=%fused_computation.240 | loop fusion | flops 35389440 | bytes 69208064 | tf_op jit(solution)/shard_map/convert_element_type | solution.py:98
  33.8 1186.6 %while.40 = (s32[]{:T(128)}, f32[1024]{0:T(1024)S(1)}, f32[1024,256]{1,0:T(8,128)}, f32[1024,256]{1,0:T(8,128)}, f32[1024,256]{1,0:T(8,128)}, /*index=5*/f32[2,2...) while((s32[]{:T(128)}, f32[1024]{0:T(1024)S(1)}, ...), condition=%wide.region_45.46_spmd.clone.clone.clone.clone, body=%wide.region_0.45_spmd.clone.clone.clone.clone.sunk | while | flops 20195917824 | bytes 935102208 | solution.py:310
  50.8 12.6 fusion.370
  63.4 25.3 %multiply_add_fusion.4 = f32[2,512,1536]{2,1,0:T(8,128)} fusion(f32[512,1536]{1,0:T(8,128)} %get-tuple-element.2286, f32[2]{0:T(128)S(1)} %get-tuple-element.2287, f32[512,1536]{1,0:T(8,128)} %get-tuple-element.2284, f32[2]{0:T(128)S(1)} %get-tuple-element.2285, f32[512,1536]{1,0:T(8,128)} %get-tuple-element.2282, f32[2]{0:T(128)S(1)} %get-tuple-element.2283, ...), kind=kLoop, calls=%fused_computation.52.clone.1 | loop fusion | flops 67633152 | bytes 75497648 | tf_op jit(solution)/shard_map/add | solution.py:96
  98.1 89.3 %all-reduce.11.cloned.1.call-done = f32[512,1024]{1,0:T(8,128)} async-done(((f32[512,1024]{1,0:T(8,128)}), f32[512,1024]{1,0:T(8,128)}) %all-reduce.11.cloned.1.call-update) | async-done | bytes 2097168 | tf_op jit(solution)/shard_map/while/body/eval_jaxpr/psum | solution.py:141
  196.0 85.6 %all-reduce.13.cloned.1.call-done = f32[512,1024]{1,0:T(8,128)} async-done(((f32[512,1024]{1,0:T(8,128)}), f32[512,1024]{1,0:T(8,128)}) %all-reduce.13.cloned.1.call-update) | async-done | bytes 2097168 | tf_op jit(solution)/shard_map/while/body/eval_jaxpr/psum | solution.py:167
  324.9 67.0 %all-reduce.15.cloned.1.call-done = f32[512,1024]{1,0:T(8,128)} async-done(((f32[512,1024]{1,0:T(8,128)}), f32[512,1024]{1,0:T(8,128)}) %all-reduce.15.cloned.1.call-update) | async-done | bytes 2097168 | tf_op jit(solution)/shard_map/while/body/eval_jaxpr/psum | solution.py:141
  415.8 73.6 %all-reduce.17.cloned.1.call-done = f32[512,1024]{1,0:T(8,128)} async-done(((f32[512,1024]{1,0:T(8,128)}), f32[512,1024]{1,0:T(8,128)}) %all-reduce.17.cloned.1.call-update) | async-done | bytes 2097168 | tf_op jit(solution)/shard_map/while/body/eval_jaxpr/psum | solution.py:195
  501.3 25.2 %fusion.382 = (f32[2]{0:T(128)}, f32[2]{0:T(128)S(1)}, f32[2]{0:T(128)S(1)}, f32[2]{0:T(128)}, f32[2]{0:T(128)}, /*index=5*/f32[2]{0:T(128)}, f32[2]{0:T(128)}, ...) fusion(pred[512,1536]{1,0:T(8,128)(4,1)S(1)} %copy-done.19, ...), kind=kLoop, calls=%fused_computation.51.clone.1 | loop fusion | flops 64487408 | bytes 29892752 | tf_op jit(solution)/shard_map/while/body/eval_jaxpr/reduce_sum | solution.py:216
  535.3 6.7 fusion.388
  547.3 10.8 psum.174
  565.9 55.6 %all-reduce.19.cloned.1.call-done = f32[512,1024]{1,0:T(8,128)} async-done(((f32[512,1024]{1,0:T(8,128)}), f32[512,1024]{1,0:T(8,128)}) %all-reduce.19.cloned.1.call-update) | async-done | bytes 2097168 | tf_op jit(solution)/shard_map/while/body/eval_jaxpr/psum | solution.py:264
  645.4 12.6 fusion.370
  658.1 25.2 %multiply_add_fusion.4 = f32[2,512,1536]{2,1,0:T(8,128)} fusion(f32[512,1536]{1,0:T(8,128)} %get-tuple-element.2286, f32[2]{0:T(128)S(1)} %get-tuple-element.2287, f32[512,1536]{1,0:T(8,128)} %get-tuple-element.2284, f32[2]{0:T(128)S(1)} %get-tuple-element.2285, f32[512,1536]{1,0:T(8,128)} %get-tuple-element.2282, f32[2]{0:T(128)S(1)} %get-tuple-element.2283, ...), kind=kLoop, calls=%fused_computation.52.clone.1 | loop fusion | flops 67633152 | bytes 75497648 | tf_op jit(solution)/shard_map/add | solution.py:96
  692.6 85.6 %all-reduce.11.cloned.1.call-done = f32[512,1024]{1,0:T(8,128)} async-done(((f32[512,1024]{1,0:T(8,128)}), f32[512,1024]{1,0:T(8,128)}) %all-reduce.11.cloned.1.call-update) | async-done | bytes 2097168 | tf_op jit(solution)/shard_map/while/body/eval_jaxpr/psum | solution.py:141
  786.8 85.6 %all-reduce.13.cloned.1.call-done = f32[512,1024]{1,0:T(8,128)} async-done(((f32[512,1024]{1,0:T(8,128)}), f32[512,1024]{1,0:T(8,128)}) %all-reduce.13.cloned.1.call-update) | async-done | bytes 2097168 | tf_op jit(solution)/shard_map/while/body/eval_jaxpr/psum | solution.py:167
  917.1 65.4 %all-reduce.15.cloned.1.call-done = f32[512,1024]{1,0:T(8,128)} async-done(((f32[512,1024]{1,0:T(8,128)}), f32[512,1024]{1,0:T(8,128)}) %all-reduce.15.cloned.1.call-update) | async-done | bytes 2097168 | tf_op jit(solution)/shard_map/while/body/eval_jaxpr/psum | solution.py:141
  1011.0 69.0 %all-reduce.17.cloned.1.call-done = f32[512,1024]{1,0:T(8,128)} async-done(((f32[512,1024]{1,0:T(8,128)}), f32[512,1024]{1,0:T(8,128)}) %all-reduce.17.cloned.1.call-update) | async-done | bytes 2097168 | tf_op jit(solution)/shard_map/while/body/eval_jaxpr/psum | solution.py:195
  1091.9 25.2 %fusion.382 = (f32[2]{0:T(128)}, f32[2]{0:T(128)S(1)}, f32[2]{0:T(128)S(1)}, f32[2]{0:T(128)}, f32[2]{0:T(128)}, /*index=5*/f32[2]{0:T(128)}, f32[2]{0:T(128)}, ...) fusion(pred[512,1536]{1,0:T(8,128)(4,1)S(1)} %copy-done.19, ...), kind=kLoop, calls=%fused_computation.51.clone.1 | loop fusion | flops 64487408 | bytes 29892752 | tf_op jit(solution)/shard_map/while/body/eval_jaxpr/reduce_sum | solution.py:216
  1125.9 6.7 fusion.388
  1137.9 10.8 psum.174
  1158.2 53.9 %all-reduce.19.cloned.1.call-done = f32[512,1024]{1,0:T(8,128)} async-done(((f32[512,1024]{1,0:T(8,128)}), f32[512,1024]{1,0:T(8,128)}) %all-reduce.19.cloned.1.call-update) | async-done | bytes 2097168 | tf_op jit(solution)/shard_map/while/body/eval_jaxpr/psum | solution.py:264
  1221.0 14.8 %all-reduce = (f32[1024]{0:T(1024)}, f32[2,22]{1,0:T(2,128)}, f32[1024]{0:T(1024)}) all-reduce(f32[1024]{0:T(1024)S(1)} %get-tuple-element.2353, f32[2,22]{1,0:T(2,128)S(1)} %get-tuple-element.2357, f32[1024]{0:T(1024)S(1)} %get-tuple-element.2359), channel_id=1, replica_groups=mesh['dp'=8,'mp'=4] {'dp'}, use_global_device_ids=true, to_apply=%region_46.47 | all-reduce | flops 2092 | bytes 16736 | tf_op jit(solution)/shard_map/psum | solution.py:311
  1235.8 187.3 %all-reduce.9.cloned.1.call-done = (f32[1024,256]{1,0:T(8,128)}, f32[1024,256]{1,0:T(8,128)}, f32[1024,256]{1,0:T(8,128)}, f32[256,1024]{1,0:T(8,128)}, f32[1024...) async-done(((f32[1024,256]{1,0:T(8,128)}, f32[1024,256]{1,0:T(8,128)}, f32[1024,256]{1,0:T(8,128)}, f32[256,1024]{1,0:T(8,128)}, f32[1024,1024]{1,0:T(8,128)}, ...) | async-done | bytes 14680080 | tf_op jit(solution)/shard_map/psum | solution.py:311
  (643 shorter events, 307.1 us)
Async XLA Ops:
  11.6 22.2 %copy-start.66 = (f32[1024]{0:T(1024)S(1)}, f32[1024]{0:T(1024)}, u32[]{:S(2)}) copy-start(f32[1024]{0:T(1024)} %param.24) | copy-start | bytes 12292
  11.6 22.2 %copy-start.71 = (f32[1024]{0:T(1024)S(1)}, f32[1024]{0:T(1024)}, u32[]{:S(2)}) copy-start(f32[1024]{0:T(1024)} %param.30) | copy-start | bytes 12292
  11.6 22.2 %copy-start.94 = (s32[2]{0:T(128)S(1)}, s32[2]{0:T(128)}, u32[]{:S(2)}) copy-start(s32[2]{0:T(128)} %param.23) | copy-start | bytes 28
  34.0 153.4 %all-reduce.11.cloned.1.call-start = ((), (), s32[]{:S(2)}) async-start(), calls=%async_computation.1 | async-start | bytes 4194304 | tf_op jit(solution)/shard_map/while/body/eval_jaxpr/psum | solution.py:141
  63.4 25.4 %copy-start.9 = (pred[512,1536]{1,0:T(8,128)(4,1)}, pred[512,1536]{1,0:T(8,128)(4,1)S(1)}, u32[]{:S(2)}) copy-start(pred[512,1536]{1,0:T(8,128)(4,1)S(1)} %get-tuple-element.1992) | copy-start | bytes 2359300 | tf_op jit(solution)/shard_map/while
  98.0 183.6 %all-reduce.13.cloned.1.call-start = ((), (), s32[]{:S(2)}) async-start(), calls=%async_computation.2 | async-start | bytes 4194304 | tf_op jit(solution)/shard_map/while/body/eval_jaxpr/psum | solution.py:167
  196.0 195.9 %all-reduce.15.cloned.1.call-start = ((), (), s32[]{:S(2)}) async-start(), calls=%async_computation.3 | async-start | bytes 4194304 | tf_op jit(solution)/shard_map/while/body/eval_jaxpr/psum | solution.py:141
  306.3 183.1 %all-reduce.17.cloned.1.call-start = ((), (), s32[]{:S(2)}) async-start(), calls=%async_computation.4 | async-start | bytes 4194304 | tf_op jit(solution)/shard_map/while/body/eval_jaxpr/psum | solution.py:195
  403.8 217.7 %all-reduce.19.cloned.1.call-start = ((), (), s32[]{:S(2)}) async-start(), calls=%async_computation.5 | async-start | bytes 4194304 | tf_op jit(solution)/shard_map/while/body/eval_jaxpr/psum | solution.py:264
  496.2 33.5 %copy-start.37 = (bf16[2,128,1536]{2,1,0:T(8,128)(2,1)}, bf16[2,128,1536]{2,1,0:T(8,128)(2,1)S(1)}, u32[]{:S(2)}) copy-start(bf16[2,128,1536]{2,1,0:T(8,128)(2,1)S(1)} %convolution_convert_fusion.27) | copy-start | bytes 2359300 | tf_op jit(solution)/shard_map/while
  501.3 25.2 %copy-start.40 = (bf16[1536,256]{0,1:T(8,128)(2,1)S(1)}, bf16[1536,256]{0,1:T(8,128)(2,1)}, u32[]{:S(2)}) copy-start(bf16[1536,256]{0,1:T(8,128)(2,1)} %copy-done.39) | copy-start | bytes 2359300 | tf_op jit(solution)/shard_map/while
  565.9 61.2 %copy-start.68 = (f32[1024,256]{1,0:T(8,128)}, f32[1024,256]{1,0:T(8,128)S(1)}, u32[]{:S(2)}) copy-start(f32[1024,256]{1,0:T(8,128)S(1)} %convolution_add_fusion.14) | copy-start | bytes 3145732 | tf_op jit(solution)/shard_map/while
  628.6 149.5 %all-reduce.11.cloned.1.call-start = ((), (), s32[]{:S(2)}) async-start(), calls=%async_computation.1 | async-start | bytes 4194304 | tf_op jit(solution)/shard_map/while/body/eval_jaxpr/psum | solution.py:141
  658.1 25.2 %copy-start.9 = (pred[512,1536]{1,0:T(8,128)(4,1)}, pred[512,1536]{1,0:T(8,128)(4,1)S(1)}, u32[]{:S(2)}) copy-start(pred[512,1536]{1,0:T(8,128)(4,1)S(1)} %get-tuple-element.1992) | copy-start | bytes 2359300 | tf_op jit(solution)/shard_map/while
  692.5 179.8 %all-reduce.13.cloned.1.call-start = ((), (), s32[]{:S(2)}) async-start(), calls=%async_computation.2 | async-start | bytes 4194304 | tf_op jit(solution)/shard_map/while/body/eval_jaxpr/psum | solution.py:167
  786.8 195.8 %all-reduce.15.cloned.1.call-start = ((), (), s32[]{:S(2)}) async-start(), calls=%async_computation.3 | async-start | bytes 4194304 | tf_op jit(solution)/shard_map/while/body/eval_jaxpr/psum | solution.py:141
  896.9 183.1 %all-reduce.17.cloned.1.call-start = ((), (), s32[]{:S(2)}) async-start(), calls=%async_computation.4 | async-start | bytes 4194304 | tf_op jit(solution)/shard_map/while/body/eval_jaxpr/psum | solution.py:195
  994.4 217.8 %all-reduce.19.cloned.1.call-start = ((), (), s32[]{:S(2)}) async-start(), calls=%async_computation.5 | async-start | bytes 4194304 | tf_op jit(solution)/shard_map/while/body/eval_jaxpr/psum | solution.py:264
  1086.8 33.5 %copy-start.37 = (bf16[2,128,1536]{2,1,0:T(8,128)(2,1)}, bf16[2,128,1536]{2,1,0:T(8,128)(2,1)S(1)}, u32[]{:S(2)}) copy-start(bf16[2,128,1536]{2,1,0:T(8,128)(2,1)S(1)} %convolution_convert_fusion.27) | copy-start | bytes 2359300 | tf_op jit(solution)/shard_map/while
  1091.9 25.2 %copy-start.40 = (bf16[1536,256]{0,1:T(8,128)(2,1)S(1)}, bf16[1536,256]{0,1:T(8,128)(2,1)}, u32[]{:S(2)}) copy-start(bf16[1536,256]{0,1:T(8,128)(2,1)} %copy-done.39) | copy-start | bytes 2359300 | tf_op jit(solution)/shard_map/while
  1135.6 16.3 %copy-start.3 = (f32[512,1024]{1,0:T(8,128)S(1)}, f32[512,1024]{1,0:T(8,128)}, u32[]{:S(2)}) copy-start(f32[512,1024]{1,0:T(8,128)} %copy-done.2) | copy-start | bytes 6291460 | tf_op jit(solution)/shard_map/while
  1135.6 16.3 %copy-start.44 = (bf16[2,128,512]{2,1,0:T(8,128)(2,1)S(1)}, bf16[2,128,512]{2,1,0:T(8,128)(2,1)}, u32[]{:S(2)}) copy-start(bf16[2,128,512]{2,1,0:T(8,128)(2,1)} %copy-done.43) | copy-start | bytes 786436 | tf_op jit(solution)/shard_map/while
  1158.2 59.5 %copy-start.68 = (f32[1024,256]{1,0:T(8,128)}, f32[1024,256]{1,0:T(8,128)S(1)}, u32[]{:S(2)}) copy-start(f32[1024,256]{1,0:T(8,128)S(1)} %convolution_add_fusion.14) | copy-start | bytes 3145732 | tf_op jit(solution)/shard_map/while
  1220.4 202.7 %all-reduce.9.cloned.1.call-start = ((), (), s32[]{:S(2)}) async-start(), calls=%async_computation | async-start | bytes 29360128 | tf_op jit(solution)/shard_map/psum | solution.py:311
  (183 other events, 656.5 us)
Sparse Core Ops, SparseCore 0:
  98.2 89.1 all-reduce.10
  196.1 85.4 all-reduce.12
  306.4 85.4 all-reduce.14
  403.9 85.4 all-reduce.16
  535.4 86.0 all-reduce.18
  692.7 85.4 all-reduce.10
  786.9 85.4 all-reduce.12
  897.0 85.4 all-reduce.14
  994.5 85.4 all-reduce.16
  1126.0 86.1 all-reduce.18
Sparse Core Ops, SparseCore 1:
  1227.0 196.1 all-reduce.8
where the time goes:
time: 1450 us
  waiting for transfers between devices  919 us (63%)
  other arithmetic  246 us (17%)
  matrix products  127 us (9%)
  local copies, waits for them, and re-layouts  94.7 us (7%)
  blocking collectives  36.4 us (3%)
  between operations  15.9 us (1%)
    psum x4, waiting for transfers between devices, attend(): attended = lax.psum(low_product(mixed_heads, output_weight), 'mp')  307 us
    psum x1, waiting for transfers between devices, body(): totals = lax.psum(totals, 'dp')  187 us
    psum x2, waiting for transfers between devices, stream_step(): branch_out = lax.psum(low_product(activated, down_weight), 'mp')  171 us
    psum x2, waiting for transfers between devices, stream_step(): grad_ffn_input = lax.psum(back_product(grad_pre, up_weight), 'mp')  143 us
    psum x2, waiting for transfers between devices, stream_step(): lax.psum((grad_unit_seg, grad_first_kept), 'mp')  110 us
    reduce_sum x4, other arithmetic, stream_step(): jnp.sum(jnp.where((distance >= mark_value)[None], score_wide, 0.0), axis=...  63.7 us
    add x2, other arithmetic, body(): bias_table + relative_bias[:, position][:, None, None] * (distance >= mar...  50.5 us
    while x380, local copies, waits for them, and re-layouts  43.6 us
  transfers between devices with their start and end apart: 11, of which 11 were waited for; matrix products, arithmetic and copies ran while one was open for 7% of the time, Pallas kernels for 0%

commit v1 on v0

--- a/solution.py
+++ b/solution.py
@@ -164,7 +164,7 @@
         )
         saved = attend(seg_rows, memory_rows, packed_rows, memory_count, packed_count)
         ffn_input, pre_act, activated = feed(saved[8])
-        branch_out = lax.psum(low_product(activated, down_weight), "mp")
+        branch_out = jnp.sum(lax.all_gather(low_product(activated, down_weight), "mp"), axis=0)
         result = (saved[8] + branch_out).astype(jnp.bfloat16)
         again = lax.optimization_barrier((seg_rows, memory_rows, packed_rows, result))
         saved = attend(again[0], again[1], again[2], memory_count, packed_count)

time: 1450 us -> 1590 us (1.097)
  waiting for transfers between devices: 919 us -> 1040 us
    all_gather x0 -> x2, waiting for transfers between devices: none -> 297 us  [stream_step(): lax.all_gather(low_product(activated, down_weight), 'mp')]
    psum x2 -> x0, waiting for transfers between devices: 171 us -> none  [stream_step(): branch_out = lax.psum(low_product(activated, down_weight), 'mp')]
  transfers between devices with their start and end apart: 11 -> 11, of which waited for: 11 -> 11; matrix products, arithmetic and copies ran while one was open for 7% -> 6% of each run, Pallas kernels for 0% -> 0%
where the time goes in v1:
time: 1590 us; the launch traced here: 1580 us
  waiting for transfers between devices  1040 us (65%)
  other arithmetic  257 us (16%)
  matrix products  127 us (8%)
  local copies, waits for them, and re-layouts  94.5 us (6%)
  blocking collectives  36.4 us (2%)
  between operations  15.9 us (1%)
    psum x4, waiting for transfers between devices, attend(): attended = lax.psum(low_product(mixed_heads, output_weight), 'mp')  306 us
    all_gather x2, waiting for transfers between devices, stream_step(): lax.all_gather(low_product(activated, down_weight), 'mp')  297 us
    psum x1, waiting for transfers between devices, body(): totals = lax.psum(totals, 'dp')  187 us
    psum x2, waiting for transfers between devices, stream_step(): grad_ffn_input = lax.psum(back_product(grad_pre, up_weight), 'mp')  143 us
    psum x2, waiting for transfers between devices, stream_step(): lax.psum((grad_unit_seg, grad_first_kept), 'mp')  109 us
    reduce_sum x4, other arithmetic, stream_step(): jnp.sum(jnp.where((distance >= mark_value)[None], score_wide, 0.0), axis=...  63.7 us
    add x2, other arithmetic, body(): bias_table + relative_bias[:, position][:, None, None] * (distance >= mar...  50.5 us
    while x380, local copies, waits for them, and re-layouts  43.5 us
  transfers between devices with their start and end apart: 11, of which 11 were waited for; matrix products, arithmetic and copies ran while one was open for 6% of the time, Pallas kernels for 0%

profile of v1, /device:TPU:0, one launch (start us, length us, event | category | flops | bytes accessed | tf_op | source)
XLA Modules:
  0.0 1581.6 jit_solution(6699587995182090438)
XLA Ops:
  11.6 21.8 %fusion.144 = (f32[512,1536]{1,0:T(8,128)}, f32[512,1536]{1,0:T(8,128)}, f32[512,1536]{1,0:T(8,128)}, f32[512,1536]{1,0:T(8,128)}, f32[512,1536]{1,0:T(8,128)}, ...) fusion(s32[512]{0:T(512)S(1)} %iota_add_fusion), kind=kLoop, calls=%fused_computation.240 | loop fusion | flops 35389440 | bytes 69208064 | tf_op jit(solution)/shard_map/convert_element_type | solution.py:98
  33.5 1322.9 %while.40 = (s32[]{:T(128)}, f32[1024]{0:T(1024)S(1)}, f32[1024,256]{1,0:T(8,128)}, f32[1024,256]{1,0:T(8,128)}, f32[1024,256]{1,0:T(8,128)}, /*index=5*/f32[2,2...) while((s32[]{:T(128)}, f32[1024]{0:T(1024)S(1)}, ...), condition=%wide.region_45.46_spmd.clone.clone.clone.clone, body=%wide.region_0.45_spmd.clone.clone.clone.clone.sunk | while | flops 20196966400 | bytes 964462336 | solution.py:310
  50.5 12.6 fusion.370
  63.1 25.3 %multiply_add_fusion.4 = f32[2,512,1536]{2,1,0:T(8,128)} fusion(f32[512,1536]{1,0:T(8,128)} %get-tuple-element.2288, f32[2]{0:T(128)S(1)} %get-tuple-element.2289, f32[512,1536]{1,0:T(8,128)} %get-tuple-element.2286, f32[2]{0:T(128)S(1)} %get-tuple-element.2287, f32[512,1536]{1,0:T(8,128)} %get-tuple-element.2284, f32[2]{0:T(128)S(1)} %get-tuple-element.2285, ...), kind=kLoop, calls=%fused_computation.52.clone.1 | loop fusion | flops 67633152 | bytes 75497648 | tf_op jit(solution)/shard_map/add | solution.py:96
  97.7 89.3 %all-reduce.10.cloned.1.call-done = f32[512,1024]{1,0:T(8,128)} async-done(((f32[512,1024]{1,0:T(8,128)}), f32[512,1024]{1,0:T(8,128)}) %all-reduce.10.cloned.1.call-update) | async-done | bytes 2097168 | tf_op jit(solution)/shard_map/while/body/eval_jaxpr/psum | solution.py:141
  195.7 148.7 %all-gather.8.cloned.1.call-done = f32[2048,1024]{1,0:T(8,128)} async-done(((f32[512,1024]{1,0:T(8,128)}), f32[2048,1024]{1,0:T(8,128)}) %all-gather.8.cloned.1.call-update) | async-done | bytes 8388624 | tf_op jit(solution)/shard_map/while/body/eval_jaxpr/all_gather | solution.py:167
  393.5 66.4 %all-reduce.12.cloned.1.call-done = f32[512,1024]{1,0:T(8,128)} async-done(((f32[512,1024]{1,0:T(8,128)}), f32[512,1024]{1,0:T(8,128)}) %all-reduce.12.cloned.1.call-update) | async-done | bytes 2097168 | tf_op jit(solution)/shard_map/while/body/eval_jaxpr/psum | solution.py:141
  483.9 73.5 %all-reduce.14.cloned.1.call-done = f32[512,1024]{1,0:T(8,128)} async-done(((f32[512,1024]{1,0:T(8,128)}), f32[512,1024]{1,0:T(8,128)}) %all-reduce.14.cloned.1.call-update) | async-done | bytes 2097168 | tf_op jit(solution)/shard_map/while/body/eval_jaxpr/psum | solution.py:195
  569.3 25.2 %fusion.382 = (f32[2]{0:T(128)}, f32[2]{0:T(128)S(1)}, f32[2]{0:T(128)S(1)}, f32[2]{0:T(128)}, f32[2]{0:T(128)}, /*index=5*/f32[2]{0:T(128)}, f32[2]{0:T(128)}, ...) fusion(pred[512,1536]{1,0:T(8,128)(4,1)S(1)} %copy-done.19, ...), kind=kLoop, calls=%fused_computation.51.clone.1 | loop fusion | flops 64487408 | bytes 29892752 | tf_op jit(solution)/shard_map/while/body/eval_jaxpr/reduce_sum | solution.py:216
  603.3 6.7 fusion.388
  615.3 10.8 psum.158
  633.9 55.6 %all-reduce.16.cloned.1.call-done = f32[512,1024]{1,0:T(8,128)} async-done(((f32[512,1024]{1,0:T(8,128)}), f32[512,1024]{1,0:T(8,128)}) %all-reduce.16.cloned.1.call-update) | async-done | bytes 2097168 | tf_op jit(solution)/shard_map/while/body/eval_jaxpr/psum | solution.py:264
  713.4 12.6 fusion.370
  726.0 25.2 %multiply_add_fusion.4 = f32[2,512,1536]{2,1,0:T(8,128)} fusion(f32[512,1536]{1,0:T(8,128)} %get-tuple-element.2288, f32[2]{0:T(128)S(1)} %get-tuple-element.2289, f32[512,1536]{1,0:T(8,128)} %get-tuple-element.2286, f32[2]{0:T(128)S(1)} %get-tuple-element.2287, f32[512,1536]{1,0:T(8,128)} %get-tuple-element.2284, f32[2]{0:T(128)S(1)} %get-tuple-element.2285, ...), kind=kLoop, calls=%fused_computation.52.clone.1 | loop fusion | flops 67633152 | bytes 75497648 | tf_op jit(solution)/shard_map/add | solution.py:96
  760.5 85.6 %all-reduce.10.cloned.1.call-done = f32[512,1024]{1,0:T(8,128)} async-done(((f32[512,1024]{1,0:T(8,128)}), f32[512,1024]{1,0:T(8,128)}) %all-reduce.10.cloned.1.call-update) | async-done | bytes 2097168 | tf_op jit(solution)/shard_map/while/body/eval_jaxpr/psum | solution.py:141
  854.8 148.7 %all-gather.8.cloned.1.call-done = f32[2048,1024]{1,0:T(8,128)} async-done(((f32[512,1024]{1,0:T(8,128)}), f32[2048,1024]{1,0:T(8,128)}) %all-gather.8.cloned.1.call-update) | async-done | bytes 8388624 | tf_op jit(solution)/shard_map/while/body/eval_jaxpr/all_gather | solution.py:167
  1054.0 64.8 %all-reduce.12.cloned.1.call-done = f32[512,1024]{1,0:T(8,128)} async-done(((f32[512,1024]{1,0:T(8,128)}), f32[512,1024]{1,0:T(8,128)}) %all-reduce.12.cloned.1.call-update) | async-done | bytes 2097168 | tf_op jit(solution)/shard_map/while/body/eval_jaxpr/psum | solution.py:141
  1147.3 69.0 %all-reduce.14.cloned.1.call-done = f32[512,1024]{1,0:T(8,128)} async-done(((f32[512,1024]{1,0:T(8,128)}), f32[512,1024]{1,0:T(8,128)}) %all-reduce.14.cloned.1.call-update) | async-done | bytes 2097168 | tf_op jit(solution)/shard_map/while/body/eval_jaxpr/psum | solution.py:195
  1228.2 25.2 %fusion.382 = (f32[2]{0:T(128)}, f32[2]{0:T(128)S(1)}, f32[2]{0:T(128)S(1)}, f32[2]{0:T(128)}, f32[2]{0:T(128)}, /*index=5*/f32[2]{0:T(128)}, f32[2]{0:T(128)}, ...) fusion(pred[512,1536]{1,0:T(8,128)(4,1)S(1)} %copy-done.19, ...), kind=kLoop, calls=%fused_computation.51.clone.1 | loop fusion | flops 64487408 | bytes 29892752 | tf_op jit(solution)/shard_map/while/body/eval_jaxpr/reduce_sum | solution.py:216
  1262.2 6.7 fusion.388
  1274.2 10.8 psum.158
  1294.5 53.6 %all-reduce.16.cloned.1.call-done = f32[512,1024]{1,0:T(8,128)} async-done(((f32[512,1024]{1,0:T(8,128)}), f32[512,1024]{1,0:T(8,128)}) %all-reduce.16.cloned.1.call-update) | async-done | bytes 2097168 | tf_op jit(solution)/shard_map/while/body/eval_jaxpr/psum | solution.py:264
  1356.9 14.8 all-reduce
  1371.8 187.3 %all-reduce.8.cloned.1.call-done = (f32[1024,256]{1,0:T(8,128)}, f32[1024,256]{1,0:T(8,128)}, f32[1024,256]{1,0:T(8,128)}, f32[256,1024]{1,0:T(8,128)}, f32[1024...) async-done(((f32[1024,256]{1,0:T(8,128)}, f32[1024,256]{1,0:T(8,128)}, f32[1024,256]{1,0:T(8,128)}, f32[256,1024]{1,0:T(8,128)}, f32[1024,1024]{1,0:T(8,128)}, ...) | async-done | bytes 14680080 | tf_op jit(solution)/shard_map/psum | solution.py:311
  (645 shorter events, 318.9 us)
Async XLA Ops:
  11.6 21.9 %copy-start.66 = (f32[1024]{0:T(1024)S(1)}, f32[1024]{0:T(1024)}, u32[]{:S(2)}) copy-start(f32[1024]{0:T(1024)} %param.24) | copy-start | bytes 12292
  11.6 21.9 %copy-start.71 = (f32[1024]{0:T(1024)S(1)}, f32[1024]{0:T(1024)}, u32[]{:S(2)}) copy-start(f32[1024]{0:T(1024)} %param.30) | copy-start | bytes 12292
  11.6 21.9 %copy-start.94 = (s32[2]{0:T(128)S(1)}, s32[2]{0:T(128)}, u32[]{:S(2)}) copy-start(s32[2]{0:T(128)} %param.23) | copy-start | bytes 28
  33.7 153.3 %all-reduce.10.cloned.1.call-start = ((), (), s32[]{:S(2)}) async-start(), calls=%async_computation.1 | async-start | bytes 4194304 | tf_op jit(solution)/shard_map/while/body/eval_jaxpr/psum | solution.py:141
  63.1 25.3 %copy-start.9 = (pred[512,1536]{1,0:T(8,128)(4,1)}, pred[512,1536]{1,0:T(8,128)(4,1)S(1)}, u32[]{:S(2)}) copy-start(pred[512,1536]{1,0:T(8,128)(4,1)S(1)} %get-tuple-element.1992) | copy-start | bytes 2359300 | tf_op jit(solution)/shard_map/while
  97.6 246.8 %all-gather.8.cloned.1.call-start = ((), (), s32[]{:S(2)}) async-start(), calls=%async_computation.2 | async-start | bytes 10485760 | tf_op jit(solution)/shard_map/while/body/eval_jaxpr/all_gather | solution.py:167
  195.7 264.3 %all-reduce.12.cloned.1.call-start = ((), (), s32[]{:S(2)}) async-start(), calls=%async_computation.3 | async-start | bytes 4194304 | tf_op jit(solution)/shard_map/while/body/eval_jaxpr/psum | solution.py:141
  375.0 182.4 %all-reduce.14.cloned.1.call-start = ((), (), s32[]{:S(2)}) async-start(), calls=%async_computation.4 | async-start | bytes 4194304 | tf_op jit(solution)/shard_map/while/body/eval_jaxpr/psum | solution.py:195
  471.8 217.7 %all-reduce.16.cloned.1.call-start = ((), (), s32[]{:S(2)}) async-start(), calls=%async_computation.5 | async-start | bytes 4194304 | tf_op jit(solution)/shard_map/while/body/eval_jaxpr/psum | solution.py:264
  564.2 33.5 %copy-start.37 = (bf16[2,128,1536]{2,1,0:T(8,128)(2,1)}, bf16[2,128,1536]{2,1,0:T(8,128)(2,1)S(1)}, u32[]{:S(2)}) copy-start(bf16[2,128,1536]{2,1,0:T(8,128)(2,1)S(1)} %convolution_convert_fusion.27) | copy-start | bytes 2359300 | tf_op jit(solution)/shard_map/while
  569.3 25.2 %copy-start.40 = (bf16[1536,256]{0,1:T(8,128)(2,1)S(1)}, bf16[1536,256]{0,1:T(8,128)(2,1)}, u32[]{:S(2)}) copy-start(bf16[1536,256]{0,1:T(8,128)(2,1)} %copy-done.39) | copy-start | bytes 2359300 | tf_op jit(solution)/shard_map/while
  633.9 61.2 %copy-start.68 = (f32[1024,256]{1,0:T(8,128)}, f32[1024,256]{1,0:T(8,128)S(1)}, u32[]{:S(2)}) copy-start(f32[1024,256]{1,0:T(8,128)S(1)} %convolution_add_fusion.14) | copy-start | bytes 3145732 | tf_op jit(solution)/shard_map/while
  696.6 149.4 %all-reduce.10.cloned.1.call-start = ((), (), s32[]{:S(2)}) async-start(), calls=%async_computation.1 | async-start | bytes 4194304 | tf_op jit(solution)/shard_map/while/body/eval_jaxpr/psum | solution.py:141
  726.0 25.2 %copy-start.9 = (pred[512,1536]{1,0:T(8,128)(4,1)}, pred[512,1536]{1,0:T(8,128)(4,1)S(1)}, u32[]{:S(2)}) copy-start(pred[512,1536]{1,0:T(8,128)(4,1)S(1)} %get-tuple-element.1992) | copy-start | bytes 2359300 | tf_op jit(solution)/shard_map/while
  760.4 243.0 %all-gather.8.cloned.1.call-start = ((), (), s32[]{:S(2)}) async-start(), calls=%async_computation.2 | async-start | bytes 10485760 | tf_op jit(solution)/shard_map/while/body/eval_jaxpr/all_gather | solution.py:167
  854.7 264.1 %all-reduce.12.cloned.1.call-start = ((), (), s32[]{:S(2)}) async-start(), calls=%async_computation.3 | async-start | bytes 4194304 | tf_op jit(solution)/shard_map/while/body/eval_jaxpr/psum | solution.py:141
  1033.9 182.4 %all-reduce.14.cloned.1.call-start = ((), (), s32[]{:S(2)}) async-start(), calls=%async_computation.4 | async-start | bytes 4194304 | tf_op jit(solution)/shard_map/while/body/eval_jaxpr/psum | solution.py:195
  1130.7 217.4 %all-reduce.16.cloned.1.call-start = ((), (), s32[]{:S(2)}) async-start(), calls=%async_computation.5 | async-start | bytes 4194304 | tf_op jit(solution)/shard_map/while/body/eval_jaxpr/psum | solution.py:264
  1223.1 33.5 %copy-start.37 = (bf16[2,128,1536]{2,1,0:T(8,128)(2,1)}, bf16[2,128,1536]{2,1,0:T(8,128)(2,1)S(1)}, u32[]{:S(2)}) copy-start(bf16[2,128,1536]{2,1,0:T(8,128)(2,1)S(1)} %convolution_convert_fusion.27) | copy-start | bytes 2359300 | tf_op jit(solution)/shard_map/while
  1228.2 25.2 %copy-start.40 = (bf16[1536,256]{0,1:T(8,128)(2,1)S(1)}, bf16[1536,256]{0,1:T(8,128)(2,1)}, u32[]{:S(2)}) copy-start(bf16[1536,256]{0,1:T(8,128)(2,1)} %copy-done.39) | copy-start | bytes 2359300 | tf_op jit(solution)/shard_map/while
  1271.9 16.3 %copy-start.3 = (f32[512,1024]{1,0:T(8,128)S(1)}, f32[512,1024]{1,0:T(8,128)}, u32[]{:S(2)}) copy-start(f32[512,1024]{1,0:T(8,128)} %copy-done.2) | copy-start | bytes 6291460 | tf_op jit(solution)/shard_map/while
  1272.0 16.2 %copy-start.44 = (bf16[2,128,512]{2,1,0:T(8,128)(2,1)S(1)}, bf16[2,128,512]{2,1,0:T(8,128)(2,1)}, u32[]{:S(2)}) copy-start(bf16[2,128,512]{2,1,0:T(8,128)(2,1)} %copy-done.43) | copy-start | bytes 786436 | tf_op jit(solution)/shard_map/while
  1294.5 59.2 %copy-start.68 = (f32[1024,256]{1,0:T(8,128)}, f32[1024,256]{1,0:T(8,128)S(1)}, u32[]{:S(2)}) copy-start(f32[1024,256]{1,0:T(8,128)S(1)} %convolution_add_fusion.14) | copy-start | bytes 3145732 | tf_op jit(solution)/shard_map/while
  1356.3 202.7 %all-reduce.8.cloned.1.call-start = ((), (), s32[]{:S(2)}) async-start(), calls=%async_computation | async-start | bytes 29360128 | tf_op jit(solution)/shard_map/psum | solution.py:311
  (183 other events, 656.6 us)
Sparse Core Ops, SparseCore 0:
  97.8 89.1 all-reduce.9
  195.8 148.5 all-gather.7
  375.2 84.7 all-reduce.11
  471.9 85.4 all-reduce.13
  603.4 86.0 all-reduce.15
  760.6 85.4 all-reduce.9
  854.8 148.5 all-gather.7
  1034.1 84.7 all-reduce.11
  1130.8 85.4 all-reduce.13
  1262.3 85.7 all-reduce.15
Sparse Core Ops, SparseCore 1:
  1362.9 196.1 all-reduce.7
